TPU v7x, 256 devices: a whole 4x4x8 slice. The times are simulated.
256 devices in a mesh: seq: 8 (over y, z_lo), exp: 32 (over x, z_hi, core).
Axes of the slice: x: 4, y: 4, z: 8 (z_hi: 4, z_lo: 2; z = z_hi * 2 + z_lo), core: 2. Of those that a mesh axis runs over, the one named last changes fastest.
Arguments:
- tokens: bfloat16 [16384, 4096], P(('seq', 'exp')), may hold values from -6 to 6
- norm_gain: float32 [4096], replicated, may hold values from 0.1 to 1.9
- queries: bfloat16 [16384, 2048], P(('seq', 'exp')), may hold values from -24 to 24
- attn_keys: bfloat16 [16384, 2048], P(('seq', 'exp')), may hold values from -4.5 to 4.5
- attn_values: bfloat16 [16384, 2048], P(('seq', 'exp')), may hold values from -6 to 6
- expert_ids: int32 [16384, 2], P(('seq', 'exp')), may hold values from 0 to 63, all different within a row; in each aligned block of 64 rows (0 to 63, 64 to 127, ...) at most 2 rows name the same one
- route_weights: float32 [16384, 2], P(('seq', 'exp')), may hold values from 0.1 to 1
- gate_proj: bfloat16 [64, 1408, 4096], P('exp', 'seq'), may hold values from -0.09375 to 0.09375
- up_proj: bfloat16 [64, 1408, 4096], P('exp', 'seq'), may hold values from -0.09375 to 0.09375
- down_proj: bfloat16 [64, 1408, 4096], P('exp', 'seq'), may hold values from -0.15625 to 0.15625
Outputs:
- attention: bfloat16 [16384, 2048], P(('seq', 'exp'))
- expert_mix: bfloat16 [16384, 4096], P(('seq', 'exp'))
Inputs may be any that keep to these rules, and one draw needn't show every extreme that they name: `expert_ids`: the two experts of a token differ. Among the rows of one device (64 consecutive tokens, aligned), every expert is named exactly 2 times.
All inputs are finite; a program needn't handle non-finite values.
Results may differ from a plain program's by a relative error of at most 0.015.
Values may be sent and summed in bfloat16 or wider, within the bound.
A program may use at most 128 MiB of HBM per device.

v0:
```python
import math
import jax
import jax.numpy as jnp
from jax import lax
from jax.sharding import PartitionSpec as P

EXPERTS = 64
HDIM = 64
SUMS = 64
SEG_DEV = 2
CAP = 2
EPS = 1e-05
NEG = -1e30


def broadcast(value, axis, source):
    kept = jnp.where(lax.axis_index(axis) == source, value, 0).astype(value.dtype)
    return lax.psum(kept, axis)


def normalize(tokens, norm_gain):
    values = tokens.astype(jnp.float32)
    inv_rms = lax.rsqrt(jnp.mean(values * values, axis=-1, keepdims=True) + EPS)
    return (values * inv_rms * norm_gain).astype(jnp.bfloat16)


def attend_block(
    query_blk, seg_keys, seg_values, sum_keys, sum_values, first_row, segment, score_scale
):
    local_sc = (
        jnp.einsum("qhd,khd->hqk", query_blk, seg_keys, preferred_element_type=jnp.float32)
        * score_scale
    )
    summ_sc = (
        jnp.einsum("qhd,khd->hqk", query_blk, sum_keys, preferred_element_type=jnp.float32)
        * score_scale
    )
    query_pos = first_row + jnp.arange(query_blk.shape[0], dtype=jnp.int32)
    key_pos = jnp.arange(seg_keys.shape[0], dtype=jnp.int32)
    local_ok = key_pos[None, :] <= query_pos[:, None]
    summ_ok = jnp.arange(sum_keys.shape[0], dtype=jnp.int32) // SUMS < segment
    local_sc = jnp.where(local_ok[None], local_sc, NEG)
    summ_sc = jnp.where(summ_ok[None, None], summ_sc, NEG)
    top_sc = jnp.maximum(
        jnp.max(local_sc, axis=-1, keepdims=True), jnp.max(summ_sc, axis=-1, keepdims=True)
    )
    local_ex = jnp.exp(local_sc - top_sc)
    summ_ex = jnp.exp(summ_sc - top_sc)
    totals = jnp.sum(local_ex, axis=-1, keepdims=True) + jnp.sum(summ_ex, axis=-1, keepdims=True)
    local_wt = (local_ex / totals).astype(jnp.bfloat16)
    summ_wt = (summ_ex / totals).astype(jnp.bfloat16)
    mixed_out = jnp.einsum("hqk,khd->qhd", local_wt, seg_values, preferred_element_type=jnp.float32)
    return mixed_out + jnp.einsum(
        "hqk,khd->qhd", summ_wt, sum_values, preferred_element_type=jnp.float32
    )


def slot_table(id_rows):
    onehot = (id_rows[..., None] == jnp.arange(EXPERTS, dtype=jnp.int32)).astype(jnp.int32)
    before = jnp.cumsum(onehot, axis=-2) - onehot
    return jnp.sum(before * onehot, axis=-1)


def fill_slots(rows, slot_pos, slot_total):
    row_count = rows.shape[0]
    padded = jnp.concatenate([rows, jnp.zeros((1, rows.shape[1]), rows.dtype)], axis=0)
    source_row = jnp.arange(row_count * 2, dtype=jnp.int32) // 2
    index_table = jnp.full((slot_total,), row_count, jnp.int32).at[slot_pos].set(source_row)
    return padded[index_table]


def expert_block(row_block, gate_proj, up_proj, down_proj):
    gate_act = jnp.einsum(
        "...ecd,efd->...ecf", row_block, gate_proj, preferred_element_type=jnp.float32
    )
    up_act = jnp.einsum(
        "...ecd,efd->...ecf", row_block, up_proj, preferred_element_type=jnp.float32
    )
    hidden = (jax.nn.silu(gate_act) * up_act).astype(jnp.bfloat16)
    return jnp.einsum("...ecf,efd->...ecd", hidden, down_proj, preferred_element_type=jnp.float32)


def on_device(
    tokens,
    norm_gain,
    queries,
    attn_keys,
    attn_values,
    expert_ids,
    route_weights,
    gate_proj,
    up_proj,
    down_proj,
):
    exp_count = lax.axis_size("exp")
    seq_count = lax.axis_size("seq")
    local_tokens = tokens.shape[0]
    feature_count = tokens.shape[1]
    normed = normalize(tokens, norm_gain)
    head_q, head_k, head_v = (
        lax.all_to_all(queries, "exp", split_axis=1, concat_axis=0, tiled=True),
        lax.all_to_all(attn_keys, "exp", split_axis=1, concat_axis=0, tiled=True),
        lax.all_to_all(attn_values, "exp", split_axis=1, concat_axis=0, tiled=True),
    )
    heads_dev = head_q.shape[1] // HDIM
    seg_len = head_q.shape[0] // SEG_DEV
    block_len = seg_len // SUMS
    head_q = head_q.reshape(SEG_DEV, seg_len, heads_dev, HDIM)
    head_k = head_k.reshape(SEG_DEV, seg_len, heads_dev, HDIM)
    head_v = head_v.reshape(SEG_DEV, seg_len, heads_dev, HDIM)
    inv_block = 1.0 / math.sqrt(block_len)
    sum_k = (
        jnp.sum(
            head_k.astype(jnp.float32).reshape(SEG_DEV, SUMS, block_len, heads_dev, HDIM), axis=2
        )
        * inv_block
    ).astype(jnp.bfloat16)
    sum_v = (
        jnp.sum(
            head_v.astype(jnp.float32).reshape(SEG_DEV, SUMS, block_len, heads_dev, HDIM), axis=2
        )
        * inv_block
    ).astype(jnp.bfloat16)
    sum_k = sum_k.reshape(SEG_DEV * SUMS, heads_dev, HDIM)
    sum_v = sum_v.reshape(SEG_DEV * SUMS, heads_dev, HDIM)
    key_list = []
    value_list = []
    for root_index in range(seq_count):
        recv_keys, recv_values = (
            broadcast(sum_k, "seq", root_index),
            broadcast(sum_v, "seq", root_index),
        )
        key_list.append(recv_keys)
        value_list.append(recv_values)
    all_keys = jnp.concatenate(key_list, axis=0)
    all_values = jnp.concatenate(value_list, axis=0)
    query_rows = min(512, seg_len)
    score_scale = 1.0 / math.sqrt(HDIM)
    seg_base = lax.axis_index("seq") * SEG_DEV
    pieces = []
    for local_seg in range(SEG_DEV):
        for first_row in range(0, seg_len, query_rows):
            block_out = attend_block(
                head_q[local_seg, first_row : first_row + query_rows],
                head_k[local_seg],
                head_v[local_seg],
                all_keys,
                all_values,
                first_row,
                seg_base + local_seg,
                score_scale,
            )
            pieces.append(block_out.astype(jnp.bfloat16))
    head_out = jnp.concatenate(pieces, axis=0).reshape(SEG_DEV * seg_len, heads_dev * HDIM)
    attention = lax.all_to_all(head_out, "exp", split_axis=0, concat_axis=1, tiled=True)
    exp_dev = EXPERTS // exp_count
    flat_ids = expert_ids.reshape(-1)
    local_pos = flat_ids * CAP + slot_table(flat_ids)
    group_normed, group_ids = (
        lax.all_gather(normed, "seq", axis=0, tiled=True),
        lax.all_gather(expert_ids, "seq", axis=0, tiled=True),
    )
    id_rows = group_ids.reshape(seq_count, local_tokens * 2)
    slot_ids = slot_table(id_rows)
    source_ids = jnp.arange(seq_count, dtype=jnp.int32)[:, None]
    owner_dev = id_rows // exp_dev
    within = id_rows % exp_dev
    slot_pos = ((owner_dev * seq_count + source_ids) * exp_dev + within) * CAP + slot_ids
    send_rows = fill_slots(group_normed, slot_pos.reshape(-1), EXPERTS * seq_count * CAP)
    send_rows = send_rows.reshape(exp_count, seq_count, exp_dev, CAP, feature_count)
    recv_rows = lax.all_to_all(send_rows, "exp", split_axis=0, concat_axis=0, tiled=True)
    slice_term = expert_block(recv_rows, gate_proj, up_proj, down_proj)
    summed = lax.psum_scatter(
        slice_term.astype(jnp.bfloat16), "seq", scatter_dimension=1, tiled=True
    )
    owner_out = summed.reshape(exp_count, exp_dev * CAP, feature_count)
    source_out = lax.all_to_all(owner_out, "exp", split_axis=0, concat_axis=0, tiled=True).reshape(
        EXPERTS * CAP, feature_count
    )
    picked = source_out[local_pos].astype(jnp.float32).reshape(local_tokens, 2, feature_count)
    expert_mix = jnp.sum(route_weights[:, :, None] * picked, axis=1).astype(jnp.bfloat16)
    return (attention, expert_mix)


def solution(mesh):
    return jax.shard_map(
        on_device,
        mesh=mesh,
        in_specs=(
            P(("seq", "exp"), None),
            P(),
            P(("seq", "exp"), None),
            P(("seq", "exp"), None),
            P(("seq", "exp"), None),
            P(("seq", "exp"), None),
            P(("seq", "exp"), None),
            P("exp", "seq", None),
            P("exp", "seq", None),
            P("exp", "seq", None),
        ),
        out_specs=(P(("seq", "exp"), None), P(("seq", "exp"), None)),
        check_vma=False,
    )
```

profile of v0, /device:TPU:33, one launch (start us, length us, event | category | flops | bytes accessed | tf_op | source)
XLA Modules:
  0.0 657.0 jit_solution(4916319611330004537)
XLA Ops:
  7.2 1.4 fusion.51
  8.7 2.0 fusion.53
  10.7 1.3 all_to_all.62
  12.1 1.2 copy.142
  13.3 1.1 reshape.872
  14.4 10.9 %all-to-all-start.2 = ((bf16[32,2,2048]{2,1,0:T(2,128)(2,1)}), bf16[32,2,2048]{2,1,0:T(2,128)(2,1)}, u32[]{:S(2)}, u32[]{:S(2)}) async-start(bf16[32,2,2048]{2,1,0:T(2,128)(2,1)} %reshape.872), calls=%async_computation.2 | async-start | bytes 524288 | tf_op jit(solution)/shard_map/all_to_all | solution.py:103
  25.3 21.3 %all-gather = s32[8,64,2]{1,2,0:T(2,128)S(1)} all-gather(s32[1,64,2]{1,2,0:T(2,128)S(1)} %bitcast.256), channel_id=1, replica_groups=mesh['seq'=8,'exp'=32] {'seq'}, dimensions={0}, use_global_device_ids=true | all-gather | bytes 4608 | tf_op jit(solution)/shard_map/all_gather | solution.py:161
  47.7 2.3 all_to_all.59
  49.9 1.2 copy.143
  51.2 1.1 reshape.868
  52.3 1.1 reshape.827
  53.4 2.5 select_reduce_fusion
  56.0 11.4 %all-to-all-start.1 = ((bf16[32,2,2048]{2,1,0:T(2,128)(2,1)}), bf16[32,2,2048]{2,1,0:T(2,128)(2,1)S(1)}, u32[]{:S(2)}, u32[]{:S(2)}) async-start(bf16[32,2,2048]{2,1,0:T(2,128)(2,1)} %reshape.868), calls=%async_computation.1 | async-start | bytes 524288 | tf_op jit(solution)/shard_map/all_to_all | solution.py:102
  67.5 4.3 scatter_custom_fusion
  71.8 45.0 %all-gather.3.cloned.1.call-done = bf16[512,4096]{1,0:T(8,128)(2,1)} async-done(((bf16[64,4096]{1,0:T(8,128)(2,1)}), bf16[512,4096]{1,0:T(8,128)(2,1)}) %all-gather.3.cloned.1.call-update) | async-done | bytes 4194320 | tf_op jit(solution)/shard_map/all_gather | solution.py:160
  116.8 4.7 concatenate.15
  121.5 17.8 %gather_fusion = bf16[1024,4096]{1,0:T(8,128)(2,1)} fusion(bf16[513,4096]{1,0:T(8,128)(2,1)} %concatenate.15, s32[1024]{0:T(1024)S(1)} %fusion.100), kind=kCustom, calls=%fused_computation | custom fusion | bytes 16781312 | tf_op jit(solution)/shard_map/gather | solution.py:69
  139.4 14.3 %reshape.828 = bf16[32,8,2,2,4096]{4,3,2,1,0:T(2,128)(2,1)} reshape(bf16[1024,4096]{1,0:T(8,128)(2,1)} %gather_fusion) | data formatting | bytes 16777216 | tf_op jit(solution)/shard_map/reshape | solution.py:170
  153.7 16.3 %copy.59 = bf16[32,8,2,2,4096]{4,1,3,2,0:T(8,128)(2,1)} copy(bf16[32,8,2,2,4096]{4,3,2,1,0:T(2,128)(2,1)} %reshape.828) | data formatting | bytes 16777216 | tf_op jit(solution)/shard_map/reshape | solution.py:170
  170.7 10.5 %all-to-all-start.4 = ((bf16[32,8,2,2,4096]{4,1,3,2,0:T(8,128)(2,1)}), bf16[32,8,2,2,4096]{4,1,3,2,0:T(8,128)(2,1)}, u32[]{:S(2)}, u32[]{:S(2)}) async-start(bf16[32,8,2,2,4096]{4,1,3,2,0:T(8,128)(2,1)} %copy.59), calls=%async_computation.4 | async-start | bytes 16777216 | tf_op jit(solution)/shard_map/all_to_all | solution.py:171
  181.3 1.3 reshape.873
  182.6 2.1 reshape.869
  184.9 1.3 convert_reduce_fusion.1
  188.7 198.8 %all-to-all-done.4 = bf16[32,8,2,2,4096]{4,1,3,2,0:T(8,128)(2,1)} async-done(((bf16[32,8,2,2,4096]{4,1,3,2,0:T(8,128)(2,1)}), bf16[32,8,2,2,4096]{4,1,3,2,0:T(8,128)(2,1)}, u32[]{:S(2)}, u32[]{:S(2)}) %all-to-all-start.4) | async-done | bytes 8388640 | tf_op jit(solution)/shard_map/all_to_all | solution.py:171
  387.6 6.7 %fusion.19 = f32[32,8,2,2,176]{4,1,3,0,2:T(8,128)S(1)} fusion(bf16[2,176,4096]{2,1,0:T(8,128)(2,1)} %param.17, bf16[32,8,2,2,4096]{4,1,3,2,0:T(8,128)(2,1)} %all-to-all-done.4), kind=kOutput, calls=%fused_computation.50 | convolution fusion | flops 1476395008 | bytes 11993088 | tf_op jit(solution)/shard_map/...ecd,efd->...ecf/dot_general | solution.py:73
  394.3 6.0 fusion.34
  400.3 5.5 convert_bitcast_fusion
  405.9 11.4 %copy.62 = bf16[32,8,2,2,4096]{4,0,3,2,1:T(8,128)(2,1)} copy(bf16[32,8,2,2,4096]{4,1,3,0,2:T(8,128)(2,1)} %convert_bitcast_fusion) | data formatting | bytes 16777216 | tf_op jit(solution)/shard_map/convert_element_type | solution.py:174
  417.2 0.9 copy-done.9
  418.4 1.1 reshape.870
  419.6 4.8 all-to-all-start
  424.4 16.2 %all-to-all-done = bf16[32,2,2048]{2,1,0:T(2,128)(2,1)S(1)} async-done(((bf16[32,2,2048]{2,1,0:T(2,128)(2,1)}), bf16[32,2,2048]{2,1,0:T(2,128)(2,1)S(1)}, u32[]{:S(2)}, u32[]{:S(2)}) %all-to-all-start) | async-done | bytes 262176 | tf_op jit(solution)/shard_map/all_to_all | solution.py:101
  442.3 1.8 fusion.118
  444.2 1.9 fusion.116
  446.1 1.9 fusion.117
  448.0 1.9 fusion.115
  449.8 0.9 constant_dynamic-update-slice_fusion.7
  468.4 1.0 fusion.57
  470.8 1.1 reshape.874
  471.9 4.3 all-to-all-start.3
  476.2 119.8 %reduce-scatter.2.cloned.1.call-done = bf16[32,1,2,2,4096]{4,0,3,2,1:T(8,128)(2,1)} async-done(((bf16[32,8,2,2,4096]{4,0,3,2,1:T(8,128)(2,1)}), bf16[32,1,2,2,4096]{4,0,3,2,1:T(8,128)(2,1)}) %reduce-scatter.2.cloned.1.call-update) | async-done | bytes 1048592 | tf_op jit(solution)/shard_map/reduce_scatter | solution.py:173
  596.0 3.0 copy.63
  599.1 9.9 %all-to-all-start.5 = ((bf16[32,4,4096]{2,1,0:T(4,128)(2,1)}), bf16[32,4,4096]{2,1,0:T(4,128)(2,1)S(1)}, u32[]{:S(2)}, u32[]{:S(2)}) async-start(bf16[32,4,4096]{2,1,0:T(4,128)(2,1)} %copy.63), calls=%async_computation.6 | async-start | bytes 2097152 | tf_op jit(solution)/shard_map/all_to_all | solution.py:177
  610.4 0.9 copy.66
  611.3 27.4 %all-to-all-done.5 = bf16[32,4,4096]{2,1,0:T(4,128)(2,1)S(1)} async-done(((bf16[32,4,4096]{2,1,0:T(4,128)(2,1)}), bf16[32,4,4096]{2,1,0:T(4,128)(2,1)S(1)}, u32[]{:S(2)}, u32[]{:S(2)}) %all-to-all-start.5) | async-done | bytes 1048608 | tf_op jit(solution)/shard_map/all_to_all | solution.py:177
  639.0 2.2 gather_fusion.1
  641.2 3.5 reshape.833
  644.7 5.6 multiply_reduce_fusion
  (136 shorter events, 26.9 us)
Async XLA Ops:
  7.2 393.1 %copy-start = (bf16[2,176,4096]{2,1,0:T(8,128)(2,1)S(1)}, bf16[2,176,4096]{2,1,0:T(8,128)(2,1)}, u32[]{:S(2)}) copy-start(bf16[2,176,4096]{2,1,0:T(8,128)(2,1)} %param.19) | copy-start | bytes 8650756
  7.2 3.6 copy-start.8
  7.2 109.6 %all-gather.3.cloned.1.call-start = ((), (), s32[]{:S(2)}) async-start(), calls=%async_computation.7 | async-start | bytes 4718592 | tf_op jit(solution)/shard_map/all_gather | solution.py:160
  10.7 14.6 %copy-start.20 = (s32[64,2]{0,1:T(2,128)S(1)}, s32[64,2]{0,1:T(2,128)}, u32[]{:S(2)}) copy-start(s32[64,2]{0,1:T(2,128)} %param.15) | copy-start | bytes 1540
  14.4 41.6 %all-to-all-start.2 = ((bf16[32,2,2048]{2,1,0:T(2,128)(2,1)}), bf16[32,2,2048]{2,1,0:T(2,128)(2,1)}, u32[]{:S(2)}, u32[]{:S(2)}) async-start(bf16[32,2,2048]{2,1,0:T(2,128)(2,1)} %reshape.872), calls=%async_computation.2 | async-start | bytes 524288 | tf_op jit(solution)/shard_map/all_to_all | solution.py:103
  56.0 114.0 %all-to-all-start.1 = ((bf16[32,2,2048]{2,1,0:T(2,128)(2,1)}), bf16[32,2,2048]{2,1,0:T(2,128)(2,1)S(1)}, u32[]{:S(2)}, u32[]{:S(2)}) async-start(bf16[32,2,2048]{2,1,0:T(2,128)(2,1)} %reshape.868), calls=%async_computation.1 | async-start | bytes 524288 | tf_op jit(solution)/shard_map/all_to_all | solution.py:102
  170.0 0.7 copy-start.7
  170.7 216.9 %all-to-all-start.4 = ((bf16[32,8,2,2,4096]{4,1,3,2,0:T(8,128)(2,1)}), bf16[32,8,2,2,4096]{4,1,3,2,0:T(8,128)(2,1)}, u32[]{:S(2)}, u32[]{:S(2)}) async-start(bf16[32,8,2,2,4096]{4,1,3,2,0:T(8,128)(2,1)} %copy.59), calls=%async_computation.4 | async-start | bytes 16777216 | tf_op jit(solution)/shard_map/all_to_all | solution.py:171
  181.2 268.6 %all-reduce.4.cloned.1.call-start = ((), (), s32[]{:S(2)}) async-start(), calls=%async_computation.9 | async-start | bytes 1048576 | tf_op jit(solution)/shard_map/psum | solution.py:18
  188.3 407.7 %reduce-scatter.2.cloned.1.call-start = ((), (), s32[]{:S(2)}) async-start(), calls=%async_computation.8 | async-start | bytes 9437184 | tf_op jit(solution)/shard_map/reduce_scatter | solution.py:173
  387.6 6.7 %copy-start.22 = (bf16[2,176,4096]{2,1,0:T(8,128)(2,1)S(1)}, bf16[2,176,4096]{2,1,0:T(8,128)(2,1)}, u32[]{:S(2)}) copy-start(bf16[2,176,4096]{2,1,0:T(8,128)(2,1)} %param.18) | copy-start | bytes 8650756
  417.2 0.9 copy-start.9
  419.6 21.1 %all-to-all-start = ((bf16[32,2,2048]{2,1,0:T(2,128)(2,1)}), bf16[32,2,2048]{2,1,0:T(2,128)(2,1)S(1)}, u32[]{:S(2)}, u32[]{:S(2)}) async-start(bf16[32,2,2048]{2,1,0:T(2,128)(2,1)} %reshape.870), calls=%async_computation | async-start | bytes 524288 | tf_op jit(solution)/shard_map/all_to_all | solution.py:101
  441.0 1.1 copy-start.2
  442.1 3.9 copy-start.10
  449.8 6.7 %copy-start.6 = (f32[512,1024]{1,0:T(8,128)S(1)}, f32[512,1024]{1,0:T(8,128)}, u32[]{:S(2)}) copy-start(f32[512,1024]{1,0:T(8,128)} %get-tuple-element.60) | copy-start | bytes 6291460
  456.1 1.0 copy-start.11
  457.1 1.6 copy-start.5
  459.2 1.6 copy-start.4
  461.3 1.6 copy-start.3
  462.9 1.1 copy-start.19
  462.9 1.1 copy-start.18
  462.9 1.1 copy-start.17
  462.9 1.2 copy-start.16
  462.9 1.2 copy-start.15
  462.9 1.2 copy-start.14
  462.9 1.2 copy-start.13
  462.9 1.2 copy-start.12
  471.9 127.2 %all-to-all-start.3 = ((bf16[32,2,2048]{2,1,0:T(2,128)(2,1)}), bf16[32,2,2048]{2,1,0:T(2,128)(2,1)S(1)}, u32[]{:S(2)}, u32[]{:S(2)}) async-start(bf16[32,2,2048]{2,1,0:T(2,128)(2,1)} %reshape.874), calls=%async_computation.3 | async-start | bytes 524288 | tf_op jit(solution)/shard_map/all_to_all | solution.py:155
  596.0 13.7 %copy-start.21 = (f32[64,2]{0,1:T(2,128)S(1)}, f32[64,2]{0,1:T(2,128)}, u32[]{:S(2)}) copy-start(f32[64,2]{0,1:T(2,128)} %param.16) | copy-start | bytes 1540
  599.1 39.7 %all-to-all-start.5 = ((bf16[32,4,4096]{2,1,0:T(4,128)(2,1)}), bf16[32,4,4096]{2,1,0:T(4,128)(2,1)S(1)}, u32[]{:S(2)}, u32[]{:S(2)}) async-start(bf16[32,4,4096]{2,1,0:T(4,128)(2,1)} %copy.63), calls=%async_computation.6 | async-start | bytes 2097152 | tf_op jit(solution)/shard_map/all_to_all | solution.py:177
  641.2 9.1 %copy-start.1 = (bf16[2,176,4096]{2,1,0:T(8,128)(2,1)S(1)}, bf16[2,176,4096]{2,1,0:T(8,128)(2,1)}, u32[]{:S(2)}) copy-start(bf16[2,176,4096]{2,1,0:T(8,128)(2,1)} %param.19) | copy-start | bytes 8650756
Sparse Core Ops, SparseCore 0:
  10.8 105.9 all-gather.2
  188.4 129.2 all-reduce.3
  417.4 178.6 reduce-scatter.1
where the time goes:
time: 666 us; the launch traced here: 657 us
  waiting for transfers between devices  407 us (61%)
  local copies, waits for them, and re-layouts  109 us (16%)
  starting transfers between devices  52.4 us (8%)
  matrix products  33.9 us (5%)
  blocking collectives  21.3 us (3%)
  other arithmetic  18.7 us (3%)
  between operations  14.7 us (2%)
    all_to_all x1, waiting for transfers between devices, on_device(): lax.all_to_all(send_rows, 'exp', split_axis=0, concat_axis=0, tiled=True)  199 us
    reduce_scatter x1, waiting for transfers between devices, on_device(): lax.psum_scatter(slice_term.astype(jnp.bfloat16), 'seq', scatter_dimensio...  120 us
    all_gather x1, waiting for transfers between devices, on_device(): lax.all_gather(normed, 'seq', axis=0, tiled=True)  45 us
    reshape x2, local copies, waits for them, and re-layouts, on_device(): send_rows.reshape(exp_count, seq_count, exp_dev, CAP, feature_count)  30.6 us
    all_to_all x1, waiting for transfers between devices, on_device(): lax.all_to_all(owner_out, 'exp', split_axis=0, concat_axis=0, tiled=True)  27.4 us
    all_gather x1, blocking collectives, on_device(): lax.all_gather(expert_ids, 'seq', axis=0, tiled=True)  21.3 us
    unnamed x72, local copies, waits for them, and re-layouts  19.5 us
    gather x1, local copies, waits for them, and re-layouts, fill_slots(): return padded[index_table]  17.8 us
  transfers between devices with their start and end apart: 9, of which 5 were waited for; matrix products, arithmetic and copies ran while one was open for 21% of the time, Pallas kernels for 0%

commit v1 on v0

--- a/solution.py
+++ b/solution.py
@@ -11,6 +11,11 @@
 CAP = 2
 EPS = 1e-05
 NEG = -1e30
+
+
+def swapped_in(x, mesh_axis, d):
+    sent = jnp.stack([x] * lax.axis_size(mesh_axis))
+    return jnp.concatenate(lax.all_to_all(sent, mesh_axis, 0, 0), axis=d)
 
 
 def broadcast(value, axis, source):
@@ -158,7 +163,7 @@
     local_pos = flat_ids * CAP + slot_table(flat_ids)
     group_normed, group_ids = (
         lax.all_gather(normed, "seq", axis=0, tiled=True),
-        lax.all_gather(expert_ids, "seq", axis=0, tiled=True),
+        swapped_in(expert_ids, "seq", 0),
     )
     id_rows = group_ids.reshape(seq_count, local_tokens * 2)
     slot_ids = slot_table(id_rows)

time: 666 us -> 666 us (level)
  waiting for transfers between devices: 407 us -> 429 us
  blocking collectives: 21.3 us -> 0 us
    all_gather x1 -> x0, blocking collectives: 21.3 us -> none  [on_device(): lax.all_gather(expert_ids, 'seq', axis=0, tiled=True)]
    all_to_all x1, waiting for transfers between devices: 0.01 us -> 10.9 us  [on_device(): lax.all_to_all(attn_values, 'exp', split_axis=1, concat_axis=0, tiled=True)]
    all_gather x1, waiting for transfers between devices: 45 us -> 55 us  [on_device(): lax.all_gather(normed, 'seq', axis=0, tiled=True)]
    all_to_all x1, starting transfers between devices: 11.4 us -> 4.49 us  [on_device(): lax.all_to_all(attn_keys, 'exp', split_axis=1, concat_axis=0, tiled=True)]
    unnamed x72 -> x75, local copies, waits for them, and re-layouts: 19.5 us -> 20.2 us
  transfers between devices with their start and end apart: 9 -> 10, of which waited for: 5 -> 7; matrix products, arithmetic and copies ran while one was open for 21% -> 21% of each run, Pallas kernels for 0% -> 0%
where the time goes in v1:
time: 666 us; the launch traced here: 657 us
  waiting for transfers between devices  429 us (64%)
  local copies, waits for them, and re-layouts  108 us (16%)
  starting transfers between devices  52.3 us (8%)
  matrix products  33.9 us (5%)
  other arithmetic  19.2 us (3%)
  between operations  14.7 us (2%)
    all_to_all x1, waiting for transfers between devices, on_device(): lax.all_to_all(send_rows, 'exp', split_axis=0, concat_axis=0, tiled=True)  199 us
    reduce_scatter x1, waiting for transfers between devices, on_device(): lax.psum_scatter(slice_term.astype(jnp.bfloat16), 'seq', scatter_dimensio...  120 us
    all_gather x1, waiting for transfers between devices, on_device(): lax.all_gather(normed, 'seq', axis=0, tiled=True)  55 us
    reshape x2, local copies, waits for them, and re-layouts, on_device(): send_rows.reshape(exp_count, seq_count, exp_dev, CAP, feature_count)  30.6 us
    all_to_all x1, waiting for transfers between devices, on_device(): lax.all_to_all(owner_out, 'exp', split_axis=0, concat_axis=0, tiled=True)  27.4 us
    unnamed x75, local copies, waits for them, and re-layouts  20.2 us
    gather x1, local copies, waits for them, and re-layouts, fill_slots(): return padded[index_table]  17.8 us
    all_to_all x1, waiting for transfers between devices, on_device(): lax.all_to_all(queries, 'exp', split_axis=1, concat_axis=0, tiled=True)  16.2 us
  transfers between devices with their start and end apart: 10, of which 7 were waited for; matrix products, arithmetic and copies ran while one was open for 21% of the time, Pallas kernels for 0%

profile of v1, /device:TPU:33, one launch (start us, length us, event | category | flops | bytes accessed | tf_op | source)
XLA Modules:
  0.0 656.9 jit_solution(3503397108101651961)
XLA Ops:
  7.2 1.4 fusion.51
  8.7 2.0 fusion.53
  11.4 5.4 all-to-all-start.4
  16.8 1.3 all_to_all.65
  18.1 1.2 copy.143
  19.3 1.1 reshape.868
  20.6 12.3 %all-to-all-start.2 = ((bf16[32,2,2048]{2,1,0:T(2,128)(2,1)}), bf16[32,2,2048]{2,1,0:T(2,128)(2,1)}, u32[]{:S(2)}, u32[]{:S(2)}) async-start(bf16[32,2,2048]{2,1,0:T(2,128)(2,1)} %reshape.868), calls=%async_computation.2 | async-start | bytes 524288 | tf_op jit(solution)/shard_map/all_to_all | solution.py:108
  33.0 2.3 all_to_all.62
  35.3 1.3 copy.144
  36.5 1.1 reshape.864
  38.9 10.9 %all-to-all-done.2 = bf16[32,2,2048]{2,1,0:T(2,128)(2,1)} async-done(((bf16[32,2,2048]{2,1,0:T(2,128)(2,1)}), bf16[32,2,2048]{2,1,0:T(2,128)(2,1)}, u32[]{:S(2)}, u32[]{:S(2)}) %all-to-all-start.2) | async-done | bytes 262176 | tf_op jit(solution)/shard_map/all_to_all | solution.py:108
  49.8 4.5 all-to-all-start.1
  54.3 2.5 select_reduce_fusion
  57.3 4.3 scatter_custom_fusion
  61.6 55.0 %all-gather.2.cloned.1.call-done = bf16[512,4096]{1,0:T(8,128)(2,1)} async-done(((bf16[64,4096]{1,0:T(8,128)(2,1)}), bf16[512,4096]{1,0:T(8,128)(2,1)}) %all-gather.2.cloned.1.call-update) | async-done | bytes 4194320 | tf_op jit(solution)/shard_map/all_gather | solution.py:165
  116.7 4.7 concatenate.15
  121.4 17.8 %gather_fusion = bf16[1024,4096]{1,0:T(8,128)(2,1)} fusion(bf16[513,4096]{1,0:T(8,128)(2,1)} %concatenate.15, s32[1024]{0:T(1024)S(1)} %fusion.100), kind=kCustom, calls=%fused_computation | custom fusion | bytes 16781312 | tf_op jit(solution)/shard_map/gather | solution.py:74
  139.2 14.3 %reshape.826 = bf16[32,8,2,2,4096]{4,3,2,1,0:T(2,128)(2,1)} reshape(bf16[1024,4096]{1,0:T(8,128)(2,1)} %gather_fusion) | data formatting | bytes 16777216 | tf_op jit(solution)/shard_map/reshape | solution.py:175
  153.5 16.3 %copy.60 = bf16[32,8,2,2,4096]{4,1,3,2,0:T(8,128)(2,1)} copy(bf16[32,8,2,2,4096]{4,3,2,1,0:T(2,128)(2,1)} %reshape.826) | data formatting | bytes 16777216 | tf_op jit(solution)/shard_map/reshape | solution.py:175
  170.5 10.5 %all-to-all-start.5 = ((bf16[32,8,2,2,4096]{4,1,3,2,0:T(8,128)(2,1)}), bf16[32,8,2,2,4096]{4,1,3,2,0:T(8,128)(2,1)}, u32[]{:S(2)}, u32[]{:S(2)}) async-start(bf16[32,8,2,2,4096]{4,1,3,2,0:T(8,128)(2,1)} %copy.60), calls=%async_computation.5 | async-start | bytes 16777216 | tf_op jit(solution)/shard_map/all_to_all | solution.py:176
  181.1 1.3 reshape.869
  182.4 2.1 reshape.865
  184.8 1.3 convert_reduce_fusion.1
  188.6 198.8 %all-to-all-done.5 = bf16[32,8,2,2,4096]{4,1,3,2,0:T(8,128)(2,1)} async-done(((bf16[32,8,2,2,4096]{4,1,3,2,0:T(8,128)(2,1)}), bf16[32,8,2,2,4096]{4,1,3,2,0:T(8,128)(2,1)}, u32[]{:S(2)}, u32[]{:S(2)}) %all-to-all-start.5) | async-done | bytes 8388640 | tf_op jit(solution)/shard_map/all_to_all | solution.py:176
  387.4 6.7 %fusion.19 = f32[32,8,2,2,176]{4,1,3,0,2:T(8,128)S(1)} fusion(bf16[2,176,4096]{2,1,0:T(8,128)(2,1)} %param.17, bf16[32,8,2,2,4096]{4,1,3,2,0:T(8,128)(2,1)} %all-to-all-done.5), kind=kOutput, calls=%fused_computation.50 | convolution fusion | flops 1476395008 | bytes 11993088 | tf_op jit(solution)/shard_map/...ecd,efd->...ecf/dot_general | solution.py:78
  394.1 6.0 fusion.34
  400.2 5.5 convert_bitcast_fusion
  405.7 11.4 %copy.63 = bf16[32,8,2,2,4096]{4,0,3,2,1:T(8,128)(2,1)} copy(bf16[32,8,2,2,4096]{4,1,3,0,2:T(8,128)(2,1)} %convert_bitcast_fusion) | data formatting | bytes 16777216 | tf_op jit(solution)/shard_map/convert_element_type | solution.py:179
  417.1 0.9 copy-done.9
  418.3 1.1 reshape.866
  419.4 4.8 all-to-all-start
  424.3 16.2 %all-to-all-done = bf16[32,2,2048]{2,1,0:T(2,128)(2,1)S(1)} async-done(((bf16[32,2,2048]{2,1,0:T(2,128)(2,1)}), bf16[32,2,2048]{2,1,0:T(2,128)(2,1)S(1)}, u32[]{:S(2)}, u32[]{:S(2)}) %all-to-all-start) | async-done | bytes 262176 | tf_op jit(solution)/shard_map/all_to_all | solution.py:106
  442.2 1.9 fusion.118
  444.0 1.9 fusion.116
  445.9 1.9 fusion.117
  447.8 1.9 fusion.115
  449.7 0.9 constant_dynamic-update-slice_fusion.7
  468.2 1.0 fusion.57
  470.6 1.1 reshape.870
  471.7 4.3 all-to-all-start.3
  476.0 119.8 %reduce-scatter.2.cloned.1.call-done = bf16[32,1,2,2,4096]{4,0,3,2,1:T(8,128)(2,1)} async-done(((bf16[32,8,2,2,4096]{4,0,3,2,1:T(8,128)(2,1)}), bf16[32,1,2,2,4096]{4,0,3,2,1:T(8,128)(2,1)}) %reduce-scatter.2.cloned.1.call-update) | async-done | bytes 1048592 | tf_op jit(solution)/shard_map/reduce_scatter | solution.py:178
  595.8 3.0 copy.64
  598.9 10.0 %all-to-all-start.6 = ((bf16[32,4,4096]{2,1,0:T(4,128)(2,1)}), bf16[32,4,4096]{2,1,0:T(4,128)(2,1)S(1)}, u32[]{:S(2)}, u32[]{:S(2)}) async-start(bf16[32,4,4096]{2,1,0:T(4,128)(2,1)} %copy.64), calls=%async_computation.7 | async-start | bytes 2097152 | tf_op jit(solution)/shard_map/all_to_all | solution.py:182
  610.3 0.9 copy.67
  611.2 27.4 %all-to-all-done.6 = bf16[32,4,4096]{2,1,0:T(4,128)(2,1)S(1)} async-done(((bf16[32,4,4096]{2,1,0:T(4,128)(2,1)}), bf16[32,4,4096]{2,1,0:T(4,128)(2,1)S(1)}, u32[]{:S(2)}, u32[]{:S(2)}) %all-to-all-start.6) | async-done | bytes 1048608 | tf_op jit(solution)/shard_map/all_to_all | solution.py:182
  638.9 2.2 gather_fusion.1
  641.0 3.5 reshape.831
  644.6 5.6 multiply_reduce_fusion
  (142 shorter events, 28.4 us)
Async XLA Ops:
  7.2 393.0 %copy-start = (bf16[2,176,4096]{2,1,0:T(8,128)(2,1)S(1)}, bf16[2,176,4096]{2,1,0:T(8,128)(2,1)}, u32[]{:S(2)}) copy-start(bf16[2,176,4096]{2,1,0:T(8,128)(2,1)} %param.19) | copy-start | bytes 8650756
  7.2 3.5 copy-start.20
  7.2 9.6 %copy-start.8 = (bf16[64,2048]{1,0:T(8,128)(2,1)S(1)}, bf16[64,2048]{1,0:T(8,128)(2,1)}, u32[]{:S(2)}) copy-start(bf16[64,2048]{1,0:T(8,128)(2,1)} %param.14) | copy-start | bytes 786436
  7.2 109.5 %all-gather.2.cloned.1.call-start = ((), (), s32[]{:S(2)}) async-start(), calls=%async_computation.8 | async-start | bytes 4718592 | tf_op jit(solution)/shard_map/all_gather | solution.py:165
  11.4 9.2 %all-to-all-start.4 = ((s32[8,1,128]{2,1,0:T(1,128)}), s32[8,1,128]{2,1,0:T(1,128)S(1)}, u32[]{:S(2)}, u32[]{:S(2)}) async-start(s32[8,1,128]{2,1,0:T(1,128)} %reshape.862), calls=%async_computation.4 | async-start | bytes 8192 | tf_op jit(solution)/shard_map/all_to_all | solution.py:18
  20.6 29.1 %all-to-all-start.2 = ((bf16[32,2,2048]{2,1,0:T(2,128)(2,1)}), bf16[32,2,2048]{2,1,0:T(2,128)(2,1)}, u32[]{:S(2)}, u32[]{:S(2)}) async-start(bf16[32,2,2048]{2,1,0:T(2,128)(2,1)} %reshape.868), calls=%async_computation.2 | async-start | bytes 524288 | tf_op jit(solution)/shard_map/all_to_all | solution.py:108
  49.8 120.0 %all-to-all-start.1 = ((bf16[32,2,2048]{2,1,0:T(2,128)(2,1)}), bf16[32,2,2048]{2,1,0:T(2,128)(2,1)S(1)}, u32[]{:S(2)}, u32[]{:S(2)}) async-start(bf16[32,2,2048]{2,1,0:T(2,128)(2,1)} %reshape.864), calls=%async_computation.1 | async-start | bytes 524288 | tf_op jit(solution)/shard_map/all_to_all | solution.py:107
  169.8 0.7 copy-start.7
  170.5 216.9 %all-to-all-start.5 = ((bf16[32,8,2,2,4096]{4,1,3,2,0:T(8,128)(2,1)}), bf16[32,8,2,2,4096]{4,1,3,2,0:T(8,128)(2,1)}, u32[]{:S(2)}, u32[]{:S(2)}) async-start(bf16[32,8,2,2,4096]{4,1,3,2,0:T(8,128)(2,1)} %copy.60), calls=%async_computation.5 | async-start | bytes 16777216 | tf_op jit(solution)/shard_map/all_to_all | solution.py:176
  181.0 268.6 %all-reduce.4.cloned.1.call-start = ((), (), s32[]{:S(2)}) async-start(), calls=%async_computation.10 | async-start | bytes 1048576 | tf_op jit(solution)/shard_map/psum | solution.py:23
  188.1 407.7 %reduce-scatter.2.cloned.1.call-start = ((), (), s32[]{:S(2)}) async-start(), calls=%async_computation.9 | async-start | bytes 9437184 | tf_op jit(solution)/shard_map/reduce_scatter | solution.py:178
  387.4 6.7 %copy-start.22 = (bf16[2,176,4096]{2,1,0:T(8,128)(2,1)S(1)}, bf16[2,176,4096]{2,1,0:T(8,128)(2,1)}, u32[]{:S(2)}) copy-start(bf16[2,176,4096]{2,1,0:T(8,128)(2,1)} %param.18) | copy-start | bytes 8650756
  417.1 0.9 copy-start.9
  419.4 21.1 %all-to-all-start = ((bf16[32,2,2048]{2,1,0:T(2,128)(2,1)}), bf16[32,2,2048]{2,1,0:T(2,128)(2,1)S(1)}, u32[]{:S(2)}, u32[]{:S(2)}) async-start(bf16[32,2,2048]{2,1,0:T(2,128)(2,1)} %reshape.866), calls=%async_computation | async-start | bytes 524288 | tf_op jit(solution)/shard_map/all_to_all | solution.py:106
  440.9 1.1 copy-start.2
  442.0 3.9 copy-start.10
  449.7 6.7 %copy-start.6 = (f32[512,1024]{1,0:T(8,128)S(1)}, f32[512,1024]{1,0:T(8,128)}, u32[]{:S(2)}) copy-start(f32[512,1024]{1,0:T(8,128)} %get-tuple-element.60) | copy-start | bytes 6291460
  455.9 1.0 copy-start.11
  456.9 1.6 copy-start.5
  459.0 1.6 copy-start.4
  461.1 1.6 copy-start.3
  462.7 1.1 copy-start.19
  462.7 1.1 copy-start.18
  462.7 1.1 copy-start.17
  462.7 1.2 copy-start.16
  462.8 1.2 copy-start.15
  462.8 1.2 copy-start.14
  462.8 1.2 copy-start.13
  462.8 1.2 copy-start.12
  471.7 127.2 %all-to-all-start.3 = ((bf16[32,2,2048]{2,1,0:T(2,128)(2,1)}), bf16[32,2,2048]{2,1,0:T(2,128)(2,1)S(1)}, u32[]{:S(2)}, u32[]{:S(2)}) async-start(bf16[32,2,2048]{2,1,0:T(2,128)(2,1)} %reshape.870), calls=%async_computation.3 | async-start | bytes 524288 | tf_op jit(solution)/shard_map/all_to_all | solution.py:160
  595.8 13.8 %copy-start.21 = (f32[64,2]{0,1:T(2,128)S(1)}, f32[64,2]{0,1:T(2,128)}, u32[]{:S(2)}) copy-start(f32[64,2]{0,1:T(2,128)} %param.16) | copy-start | bytes 1540
  598.9 39.7 %all-to-all-start.6 = ((bf16[32,4,4096]{2,1,0:T(4,128)(2,1)}), bf16[32,4,4096]{2,1,0:T(4,128)(2,1)S(1)}, u32[]{:S(2)}, u32[]{:S(2)}) async-start(bf16[32,4,4096]{2,1,0:T(4,128)(2,1)} %copy.64), calls=%async_computation.7 | async-start | bytes 2097152 | tf_op jit(solution)/shard_map/all_to_all | solution.py:182
  641.0 9.1 %copy-start.1 = (bf16[2,176,4096]{2,1,0:T(8,128)(2,1)S(1)}, bf16[2,176,4096]{2,1,0:T(8,128)(2,1)}, u32[]{:S(2)}) copy-start(bf16[2,176,4096]{2,1,0:T(8,128)(2,1)} %param.19) | copy-start | bytes 8650756
Sparse Core Ops, SparseCore 0:
  10.8 105.7 all-gather.1
  188.2 129.1 all-reduce.3
  417.2 178.5 reduce-scatter.1
